TPU v7x, 32 devices: a whole 2x2x4 slice. The times are simulated.
32 devices in a mesh: groups: 2 (over x), wide: 16 (over z, y, core).
Axes of the slice: x: 2, y: 2, z: 4, core: 2. Of those that a mesh axis runs over, the one named last changes fastest.
Arguments:
- prefix_hidden: bfloat16 [32, 256, 8192], P(('groups', 'wide')), parts along dimension 0, may hold values from -6 to 6
- prefix_lengths: int32 [32], P(('groups', 'wide')), parts along dimension 0, may hold values from 64 to 256
- action_noise: float32 [32, 50, 32], P(('groups', 'wide')), parts along dimension 0, may hold values from -4 to 4
- prefix_gain: float32 [8192], replicated, may hold values from 0.1 to 1.9
- key_weight: bfloat16 [8192, 512], P('wide'), may hold values from -0.0625 to 0.0625
- value_weight: bfloat16 [8192, 512], P('wide'), may hold values from -0.0625 to 0.0625
- input_weight: float32 [32, 1024], replicated, may hold values from -1 to 1
- expert_gain: float32 [1024], replicated, may hold values from 0.1 to 1.9
- expert_query: bfloat16 [1024, 1024], P('wide'), may hold values from -0.1875 to 0.1875
- expert_key: bfloat16 [1024, 512], P('wide'), may hold values from -5.3125 to 5.3125
- expert_value: bfloat16 [1024, 512], P('wide'), may hold values from -0.1875 to 0.1875
- expert_output: bfloat16 [1024, 1024], P('wide'), may hold values from -0.1875 to 0.1875
- final_gain: float32 [1024], replicated, may hold values from 0.1 to 1.9
- output_weight: bfloat16 [1024, 32], replicated, may hold values from -0.1875 to 0.1875
Outputs:
- actions: float32 [32, 50, 32], P(('groups', 'wide')), parts along dimension 0
There are 2 independent parts, one for each index of `groups`. A program takes and returns all parts, laid end to end along the dimension named above; an argument that names none is the same for every part. Nothing has to cross between parts.
Inputs may be any that keep to these rules, and one draw needn't show every extreme that they name: `prefix_lengths`: positions at or after a sample's length are padding and take no part.
All inputs are finite; a program needn't handle non-finite values.
Results may differ from a plain program's by a relative error of at most 0.0075.
Values may be sent and summed in bfloat16 or wider, within the bound.
A program may use at most 128 MiB of HBM per device.

v0:
```python
import jax
import jax.numpy as jnp
from jax import lax
from jax.sharding import PartitionSpec as P

HEAD = 128
STEPS = 4
rope_base = 1000000.0
norm_eps = 1e-06


def normalize(values, norm_gain):
    mean_square = jnp.mean(values * values, axis=-1, keepdims=True)
    return values * lax.rsqrt(mean_square + norm_eps) * norm_gain


def rotate(values, positions):
    half_width = values.shape[-1] // 2
    inv_freqs = rope_base ** (-jnp.arange(half_width, dtype=jnp.float32) * 2.0 / values.shape[-1])
    angles = positions[:, None] * inv_freqs[None, :]
    cosine = jnp.cos(angles)[:, None, :]
    sine_part = jnp.sin(angles)[:, None, :]
    first_half = values[..., :half_width]
    second = values[..., half_width:]
    return jnp.concatenate(
        [first_half * cosine - second * sine_part, second * cosine + first_half * sine_part], -1
    )


def time_embedding(time_value, embed_width):
    half_width = embed_width // 2
    fraction = jnp.arange(half_width, dtype=jnp.float32) / (half_width - 1)
    period = 0.004 * (4.0 / 0.004) ** fraction
    angles = time_value * (2.0 * jnp.pi) / period
    return jnp.concatenate([jnp.sin(angles), jnp.cos(angles)])


def attend(queries, key_cache, value_cache, action_keys, action_values, is_valid):
    span_rows = queries.shape[0]
    groups = key_cache.shape[1] // HEAD
    group_ratio = queries.shape[1] // key_cache.shape[1]
    query_heads = queries.reshape(span_rows, groups, group_ratio, HEAD)
    prefix_keys = key_cache.reshape(-1, groups, HEAD)
    prefix_values = value_cache.reshape(-1, groups, HEAD)
    own_keys = action_keys.reshape(span_rows, groups, HEAD)
    own_values = action_values.reshape(span_rows, groups, HEAD)
    prefix_scores = jnp.einsum(
        "cgrh,pgh->grcp", query_heads, prefix_keys, preferred_element_type=jnp.float32
    )
    prefix_scores = jnp.where(is_valid[None, None, None, :], prefix_scores, -1e30)
    own_scores = jnp.einsum(
        "cgrh,ngh->grcn", query_heads, own_keys, preferred_element_type=jnp.float32
    )
    row_max = jnp.maximum(jnp.max(prefix_scores, -1), jnp.max(own_scores, -1))[..., None]
    prefix_exp = jnp.exp(prefix_scores - row_max)
    own_exp = jnp.exp(own_scores - row_max)
    prob_total = jnp.sum(prefix_exp, -1, keepdims=True) + jnp.sum(own_exp, -1, keepdims=True)
    prefix_prob = (prefix_exp / prob_total).astype(jnp.bfloat16)
    own_prob = (own_exp / prob_total).astype(jnp.bfloat16)
    attn_mixed = jnp.einsum(
        "grcp,pgh->cgrh", prefix_prob, prefix_values, preferred_element_type=jnp.float32
    )
    attn_mixed = attn_mixed + jnp.einsum(
        "grcn,ngh->cgrh", own_prob, own_values, preferred_element_type=jnp.float32
    )
    return attn_mixed.reshape(span_rows, -1).astype(jnp.bfloat16)


def expert_steps(
    noise_rows,
    length,
    input_weight,
    expert_gain,
    query_w,
    key_w,
    value_w,
    output_w,
    final_gain,
    output_weight,
    key_cache,
    value_cache,
):
    span_rows = noise_rows.shape[0]
    is_valid = jnp.arange(key_cache.shape[0], dtype=jnp.int32) < length
    positions = length.astype(jnp.float32) + jnp.arange(span_rows, dtype=jnp.float32)
    action_state = noise_rows
    for step_idx in range(STEPS):
        time_value = 1.0 - step_idx / STEPS
        hidden = jnp.dot(
            action_state,
            input_weight,
            precision=lax.Precision.HIGHEST,
            preferred_element_type=jnp.float32,
        )
        hidden = hidden + time_embedding(time_value, input_weight.shape[1])[None, :]
        normed = normalize(hidden, expert_gain).astype(jnp.bfloat16)
        raw_queries = jnp.dot(normed, query_w, preferred_element_type=jnp.float32)
        queries = rotate(raw_queries.reshape(span_rows, -1, HEAD), positions).reshape(span_rows, -1)
        queries = (queries * HEAD ** (-0.5)).astype(jnp.bfloat16)
        raw_keys = jnp.dot(normed, key_w, preferred_element_type=jnp.float32)
        action_keys = (
            rotate(raw_keys.reshape(span_rows, -1, HEAD), positions)
            .reshape(span_rows, -1)
            .astype(jnp.bfloat16)
        )
        action_values = jnp.dot(normed, value_w, preferred_element_type=jnp.float32).astype(
            jnp.bfloat16
        )
        attn_mixed = attend(queries, key_cache, value_cache, action_keys, action_values, is_valid)
        hidden = hidden + jnp.dot(attn_mixed, output_w, preferred_element_type=jnp.float32)
        final_normed = normalize(hidden, final_gain).astype(jnp.bfloat16)
        velocity = jnp.dot(final_normed, output_weight, preferred_element_type=jnp.float32)
        action_state = action_state - velocity / STEPS
    return action_state


def shards(
    prefix_hidden,
    prefix_lengths,
    action_noise,
    prefix_gain,
    key_weight,
    value_weight,
    input_weight,
    expert_gain,
    expert_query,
    expert_key,
    expert_value,
    expert_output,
    final_gain,
    output_weight,
):
    gathered = (
        lax.all_gather(expert_query, "wide", axis=0, tiled=True),
        lax.all_gather(expert_key, "wide", axis=0, tiled=True),
        lax.all_gather(expert_value, "wide", axis=0, tiled=True),
        lax.all_gather(expert_output, "wide", axis=0, tiled=True),
    )
    hidden = prefix_hidden[0]
    row_count = hidden.shape[0]
    normed = normalize(hidden.astype(jnp.float32), prefix_gain).astype(jnp.bfloat16)
    stacked = jnp.stack([key_weight, value_weight], 0)
    projected = jnp.einsum(
        "pd,kdc->pkc",
        normed,
        lax.all_gather(stacked, "wide", axis=1, tiled=True),
        preferred_element_type=jnp.float32,
    )
    positions = jnp.arange(row_count, dtype=jnp.float32)
    key_cache = (
        rotate(projected[:, 0].reshape(row_count, -1, HEAD), positions)
        .reshape(row_count, -1)
        .astype(jnp.bfloat16)
    )
    value_cache = projected[:, 1].astype(jnp.bfloat16)
    query_w, key_w, value_w, output_w = gathered
    action_state = expert_steps(
        action_noise[0],
        prefix_lengths[0],
        input_weight,
        expert_gain,
        query_w,
        key_w,
        value_w,
        output_w,
        final_gain,
        output_weight,
        key_cache,
        value_cache,
    )
    return action_state[None]


def solution(mesh):
    placed = (
        P(("groups", "wide"), None, None),
        P(("groups", "wide")),
        P(("groups", "wide"), None, None),
        P(),
        P("wide", None),
        P("wide", None),
        P(),
        P(),
        P("wide", None),
        P("wide", None),
        P("wide", None),
        P("wide", None),
        P(),
        P(),
    )
    return jax.shard_map(
        shards,
        mesh=mesh,
        in_specs=placed,
        out_specs=P(("groups", "wide"), None, None),
        check_vma=False,
    )
```

profile of v0, /device:TPU:0, one launch (start us, length us, event | category | flops | bytes accessed | tf_op | source)
XLA Modules:
  0.0 368.0 jit_solution(7898720133912089493)
XLA Ops:
  6.5 0.7 all-gather.10.cloned.1.call-update
  7.3 0.7 all-gather.12.cloned.1.call-update
  8.1 0.7 all-gather.8.cloned.1.call-update
  8.8 2.3 pad_maximum_fusion
  11.1 0.5 all-gather.14.cloned.1.call-update
  12.0 3.1 fusion
  15.1 0.5 fusion.47
  17.1 0.6 pad_maximum_fusion.2
  17.7 0.6 pad_maximum_fusion.3
  18.3 0.6 pad_maximum_fusion.4
  19.0 31.2 %all-gather.10.cloned.1.call-done = bf16[1024,512]{1,0:T(8,128)(2,1)} async-done(((bf16[64,512]{1,0:T(8,128)(2,1)}), bf16[1024,512]{1,0:T(8,128)(2,1)}) %all-gather.10.cloned.1.call-update) | async-done | bytes 1048592 | tf_op jit(solution)/shard_map/all_gather | solution.py:135
  50.2 1.5 fusion.107
  51.9 37.4 %all-gather.12.cloned.1.call-done = bf16[1024,512]{1,0:T(8,128)(2,1)} async-done(((bf16[64,512]{1,0:T(8,128)(2,1)}), bf16[1024,512]{1,0:T(8,128)(2,1)}) %all-gather.12.cloned.1.call-update) | async-done | bytes 1048592 | tf_op jit(solution)/shard_map/all_gather | solution.py:136
  89.2 1.5 convolution_convert_fusion.3
  90.7 0.6 reshape.309
  91.4 40.4 %all-gather.8.cloned.1.call-done = bf16[1024,1024]{1,0:T(8,128)(2,1)} async-done(((bf16[64,1024]{1,0:T(8,128)(2,1)}), bf16[1024,1024]{1,0:T(8,128)(2,1)}) %all-gather.8.cloned.1.call-update) | async-done | bytes 2097168 | tf_op jit(solution)/shard_map/all_gather | solution.py:134
  131.9 2.1 fusion.106
  134.6 124.5 %all-gather.6.cloned.1.call-done = bf16[2,8192,512]{2,1,0:T(8,128)(2,1)} async-done(((bf16[2,512,512]{2,1,0:T(8,128)(2,1)}), bf16[2,8192,512]{2,1,0:T(8,128)(2,1)}) %all-gather.6.cloned.1.call-update) | async-done | bytes 16777232 | tf_op jit(solution)/shard_map/all_gather | solution.py:146
  259.1 9.5 %fusion.4 = f32[256,2,512]{2,0,1:T(8,128)S(1)} fusion(bf16[2,8192,512]{2,1,0:T(8,128)(2,1)} %all-gather.6.cloned.1.call-done, bf16[1,256,8192]{2,1,0:T(8,128)(2,1)} %param.14, f32[8192]{0:T(1024)S(1)} %copy-done.58, f32[256]{0:T(256)S(1)} %add_rsqrt_fusion), kind=kOutput, calls=%fused_computation.6 | convolution fusion | flops 4303355904 | bytes 22053888 | tf_op jit(solution)/shard_map/pd,kdc->pkc/dot_general | solution.py:143
  271.2 29.5 %all-gather.14.cloned.1.call-done = bf16[1024,1024]{1,0:T(8,128)(2,1)} async-done(((bf16[64,1024]{1,0:T(8,128)(2,1)}), bf16[1024,1024]{1,0:T(8,128)(2,1)}) %all-gather.14.cloned.1.call-update) | async-done | bytes 2097168 | tf_op jit(solution)/shard_map/all_gather | solution.py:137
  300.8 2.2 multiply_reduce_fusion.6
  303.9 0.6 copy-done.21
  305.3 0.6 copy-done.34
  306.0 1.7 fusion.100
  307.7 0.9 fusion.109
  308.6 1.6 reshape.311
  310.2 1.1 fusion.96
  311.3 0.8 subtract_convert_fusion.3
  312.1 1.2 fusion.101
  313.3 0.7 max.29
  314.1 1.3 fusion.27
  315.5 2.1 fusion.31
  317.6 0.9 convolution_convert_fusion.2
  318.5 1.5 reshape.312
  320.0 1.3 fusion.19
  321.3 0.7 copy.50
  322.0 1.6 convert_element_type.174
  323.6 2.2 multiply_reduce_fusion.4
  326.7 0.7 copy-done.22
  328.4 0.6 copy-done.35
  329.0 1.1 fusion.102
  330.1 0.9 fusion.111
  331.1 1.6 reshape.314
  332.6 1.1 fusion.95
  333.7 0.8 subtract_convert_fusion.2
  334.5 1.2 fusion.103
  335.7 1.4 fusion.28
  337.2 2.1 fusion.32
  339.3 0.9 convolution_convert_fusion.1
  340.2 1.5 reshape.315
  341.7 1.3 fusion.18
  343.0 0.7 copy.57
  343.7 1.6 convert_element_type.184
  345.3 2.2 multiply_reduce_fusion.2
  347.6 1.0 fusion.23
  348.6 1.2 multiply_reduce_fusion.1
  349.8 0.7 copy-done.19
  350.5 0.8 multiply_convert_fusion.1
  354.5 2.3 fusion.33
  356.7 0.9 convolution_convert_fusion
  357.7 0.9 reshape.318
  358.5 1.3 fusion.17
  360.0 0.6 multiply_reduce_fusion
  360.6 0.8 fusion.22
  (205 shorter events, 11.1 us)
Async XLA Ops:
  6.5 9.1 %copy-start = (f32[32,1024]{1,0:T(8,128)S(1)}, f32[32,1024]{1,0:T(8,128)}, u32[]{:S(2)}) copy-start(f32[32,1024]{1,0:T(8,128)} %param.20) | copy-start | bytes 393220
  6.5 43.7 %all-gather.10.cloned.1.call-start = ((), (), s32[]{:S(2)}) async-start(), calls=%async_computation.2 | async-start | bytes 1114112 | tf_op jit(solution)/shard_map/all_gather | solution.py:135
  7.3 82.0 %all-gather.12.cloned.1.call-start = ((), (), s32[]{:S(2)}) async-start(), calls=%async_computation.3 | async-start | bytes 1114112 | tf_op jit(solution)/shard_map/all_gather | solution.py:136
  8.0 123.8 %all-gather.8.cloned.1.call-start = ((), (), s32[]{:S(2)}) async-start(), calls=%async_computation.1 | async-start | bytes 2228224 | tf_op jit(solution)/shard_map/all_gather | solution.py:134
  8.7 250.4 %all-gather.6.cloned.1.call-start = ((), (), s32[]{:S(2)}) async-start(), calls=%async_computation | async-start | bytes 17825792 | tf_op jit(solution)/shard_map/all_gather | solution.py:146
  11.1 289.7 %all-gather.14.cloned.1.call-start = ((), (), s32[]{:S(2)}) async-start(), calls=%async_computation.4 | async-start | bytes 2228224 | tf_op jit(solution)/shard_map/all_gather | solution.py:137
  11.9 3.7 %copy-start.44 = (f32[1,50,32]{1,2,0:T(8,128)S(1)}, f32[1,50,32]{1,2,0:T(8,128)}, u32[]{:S(2)}) copy-start(f32[1,50,32]{1,2,0:T(8,128)} %param.16) | copy-start | bytes 19204
  12.0 6.9 %copy-start.41 = (f32[1024]{0:T(1024)S(1)}, f32[1024]{0:T(1024)}, u32[]{:S(2)}) copy-start(f32[1024]{0:T(1024)} %param.21) | copy-start | bytes 12292
  16.1 117.8 %copy-start.17 = (f32[50,1024]{1,0:T(8,128)}, f32[50,1024]{1,0:T(8,128)S(1)}, u32[]{:S(2)}) copy-start(f32[50,1024]{1,0:T(8,128)S(1)} %get-tuple-element.38) | copy-start | bytes 614404
  17.0 117.0 %copy-start.7 = (f32[50,64]{1,0:T(8,128)}, f32[50,64]{1,0:T(8,128)S(1)}, u32[]{:S(2)}) copy-start(f32[50,64]{1,0:T(8,128)S(1)} %get-tuple-element.33) | copy-start | bytes 38404
  17.0 117.0 %copy-start.12 = (f32[50,64]{1,0:T(8,128)}, f32[50,64]{1,0:T(8,128)S(1)}, u32[]{:S(2)}) copy-start(f32[50,64]{1,0:T(8,128)S(1)} %get-tuple-element.34) | copy-start | bytes 38404
  17.0 252.6 %copy-start.53 = (pred[256]{0:T(512)(128)(4,1)}, pred[256]{0:T(512)(128)(4,1)S(1)}, u32[]{:S(2)}) copy-start(pred[256]{0:T(512)(128)(4,1)S(1)} %iota_compare_fusion) | copy-start | bytes 772
  91.4 167.7 %copy-start.58 = (f32[8192]{0:T(1024)S(1)}, f32[8192]{0:T(1024)}, u32[]{:S(2)}) copy-start(f32[8192]{0:T(1024)} %param.17) | copy-start | bytes 98308
  269.0 1.4 copy-start.39
  269.7 1.1 copy-start.49
  270.1 30.6 %copy-start.18 = (f32[50,1024]{1,0:T(8,128)S(1)}, f32[50,1024]{1,0:T(8,128)}, u32[]{:S(2)}) copy-start(f32[50,1024]{1,0:T(8,128)} %copy-done.17) | copy-start | bytes 614404
  270.8 32.2 %copy-start.30 = (bf16[1024,32]{0,1:T(8,128)(2,1)S(1)}, bf16[1024,32]{0,1:T(8,128)(2,1)}, u32[]{:S(2)}) copy-start(bf16[1024,32]{0,1:T(8,128)(2,1)} %param.27) | copy-start | bytes 196612
  270.8 32.2 %copy-start.45 = (f32[1,50,32]{1,2,0:T(8,128)S(1)}, f32[1,50,32]{1,2,0:T(8,128)}, u32[]{:S(2)}) copy-start(f32[1,50,32]{1,2,0:T(8,128)} %param.16) | copy-start | bytes 19204
  270.8 32.2 %copy-start.46 = (f32[1024]{0:T(1024)S(1)}, f32[1024]{0:T(1024)}, u32[]{:S(2)}) copy-start(f32[1024]{0:T(1024)} %param.26) | copy-start | bytes 12292
  270.8 32.4 %copy-start.52 = (f32[1024]{0:T(1024)S(1)}, f32[1024]{0:T(1024)}, u32[]{:S(2)}) copy-start(f32[1024]{0:T(1024)} %pad_maximum_fusion.2) | copy-start | bytes 12292
  271.1 32.7 %copy-start.42 = (f32[1024]{0:T(1024)S(1)}, f32[1024]{0:T(1024)}, u32[]{:S(2)}) copy-start(f32[1024]{0:T(1024)} %param.21) | copy-start | bytes 12292
  271.1 33.4 %copy-start.1 = (bf16[1024,1024]{1,0:T(8,128)(2,1)S(1)}, bf16[1024,1024]{1,0:T(8,128)(2,1)}, u32[]{:S(2)}) copy-start(bf16[1024,1024]{1,0:T(8,128)(2,1)} %all-gather.8.cloned.1.call-done) | copy-start | bytes 6291460
  303.2 1.8 copy-start.8
  303.2 1.8 copy-start.13
  303.7 0.7 copy-start.21
  304.4 3.2 copy-start.25
  304.4 1.5 copy-start.54
  304.9 2.7 copy-start.4
  305.3 0.7 copy-start.34
  310.2 7.4 %copy-start.3 = (bf16[1024,512]{1,0:T(8,128)(2,1)S(1)}, bf16[1024,512]{1,0:T(8,128)(2,1)}, u32[]{:S(2)}) copy-start(bf16[1024,512]{1,0:T(8,128)(2,1)} %all-gather.12.cloned.1.call-done) | copy-start | bytes 3145732
  310.2 7.4 %copy-start.26 = (bf16[50,1024]{1,0:T(8,128)(2,1)S(1)}, bf16[50,1024]{1,0:T(8,128)(2,1)}, u32[]{:S(2)}) copy-start(bf16[50,1024]{1,0:T(8,128)(2,1)} %copy-done.25) | copy-start | bytes 307204
  313.3 2.0 copy-start.37
  314.1 1.4 copy-start.50
  315.4 2.1 copy-start.57
  323.6 2.3 copy-start.31
  323.6 2.3 copy-start.47
  323.6 2.5 copy-start.51
  323.6 3.7 %copy-start.43 = (f32[1024]{0:T(1024)S(1)}, f32[1024]{0:T(1024)}, u32[]{:S(2)}) copy-start(f32[1024]{0:T(1024)} %param.21) | copy-start | bytes 12292
  326.1 1.9 copy-start.40
  326.2 1.9 copy-start.9
  326.2 1.9 copy-start.14
  326.7 0.7 copy-start.22
  327.4 2.7 copy-start.27
  327.5 1.6 copy-start.55
  327.9 2.2 copy-start.5
  328.4 0.7 copy-start.35
  332.6 6.7 %copy-start.28 = (bf16[50,1024]{1,0:T(8,128)(2,1)S(1)}, bf16[50,1024]{1,0:T(8,128)(2,1)}, u32[]{:S(2)}) copy-start(bf16[50,1024]{1,0:T(8,128)(2,1)} %copy-done.27) | copy-start | bytes 307204
  335.7 1.4 copy-start.38
  345.3 2.2 copy-start.32
  348.5 3.3 copy-start.10
  348.5 3.3 copy-start.15
  349.7 0.7 copy-start.19
  351.2 1.3 copy-start.23
  351.2 0.9 copy-start.56
  351.7 1.2 copy-start.6
  351.8 1.6 copy-start.11
  351.9 1.6 copy-start.16
  353.0 1.2 copy-start.29
  353.3 3.4 copy-start.24
  353.8 0.7 copy-start.36
  354.5 5.5 %copy-start.2 = (bf16[1024,1024]{1,0:T(8,128)(2,1)S(1)}, bf16[1024,1024]{1,0:T(8,128)(2,1)}, u32[]{:S(2)}) copy-start(bf16[1024,1024]{1,0:T(8,128)(2,1)} %all-gather.14.cloned.1.call-done) | copy-start | bytes 6291460
  354.5 5.5 %copy-start.20 = (f32[50,1024]{1,0:T(8,128)S(1)}, f32[50,1024]{1,0:T(8,128)}, u32[]{:S(2)}) copy-start(f32[50,1024]{1,0:T(8,128)} %copy-done.19) | copy-start | bytes 614404
  357.6 2.9 copy-start.33
  357.6 2.9 copy-start.48
Sparse Core Ops, SparseCore 0:
  9.5 40.6 all-gather.9
  52.4 36.8 all-gather.11
  91.4 40.4 all-gather.7
  133.9 125.1 all-gather.5
  261.1 39.6 all-gather.13
where the time goes:
time: 369 us; the launch traced here: 368 us
  waiting for transfers between devices  266 us (72%)
  matrix products  50.5 us (14%)
  local copies, waits for them, and re-layouts  20.1 us (5%)
  other arithmetic  16.4 us (4%)
  between operations  15.1 us (4%)
    all_gather x1, waiting for transfers between devices, shards(): lax.all_gather(stacked, 'wide', axis=1, tiled=True)  124 us
    all_gather x1, waiting for transfers between devices, shards(): lax.all_gather(expert_query, 'wide', axis=0, tiled=True)  40.4 us
    all_gather x1, waiting for transfers between devices, shards(): lax.all_gather(expert_value, 'wide', axis=0, tiled=True)  37.4 us
    all_gather x1, waiting for transfers between devices, shards(): lax.all_gather(expert_key, 'wide', axis=0, tiled=True)  31.2 us
    all_gather x1, waiting for transfers between devices, shards(): lax.all_gather(expert_output, 'wide', axis=0, tiled=True)  29.5 us
    dot_general x1, matrix products, shards(): jnp.einsum('pd,kdc->pkc', normed, lax.all_gather(stacked, 'wide', axis=1,...  9.54 us
  transfers between devices with their start and end apart: 5, of which 5 were waited for; matrix products, arithmetic and copies ran while one was open for 7% of the time, Pallas kernels for 0%

commit v1 on v0

--- a/solution.py
+++ b/solution.py
@@ -7,6 +7,18 @@
 STEPS = 4
 rope_base = 1000000.0
 norm_eps = 1e-06
+
+
+def collect(x, axis, dim):
+    ways, here, step = (lax.axis_size(axis), lax.axis_index(axis), x.shape[dim])
+    line, have = (x, 1)
+    while have < ways:
+        line = jnp.concatenate(
+            [line, lax.ppermute(line, axis, [(d, (d - have) % ways) for d in range(ways)])],
+            axis=dim,
+        )
+        have = 2 * have
+    return jnp.roll(line, here * step, axis=dim)
 
 
 def normalize(values, norm_gain):
@@ -133,7 +145,7 @@
     gathered = (
         lax.all_gather(expert_query, "wide", axis=0, tiled=True),
         lax.all_gather(expert_key, "wide", axis=0, tiled=True),
-        lax.all_gather(expert_value, "wide", axis=0, tiled=True),
+        collect(expert_value, "wide", 0),
         lax.all_gather(expert_output, "wide", axis=0, tiled=True),
     )
     hidden = prefix_hidden[0]

time: 369 us -> 347 us (0.940)
  waiting for transfers between devices: 266 us -> 238 us
  starting transfers between devices: 0.16 us -> 8.38 us
    ppermute x0 -> x4, waiting for transfers between devices: none -> 38.6 us  [collect(): lax.ppermute(line, axis, [(d, (d - have) % ways) for d in range(ways)])]
    all_gather x1 -> x0, waiting for transfers between devices: 37.4 us -> none  [shards(): lax.all_gather(expert_value, 'wide', axis=0, tiled=True)]
    all_gather x1, waiting for transfers between devices: 31.2 us -> 0.54 us  [shards(): lax.all_gather(expert_key, 'wide', axis=0, tiled=True)]
    ppermute x0 -> x4, starting transfers between devices: none -> 8.26 us  [collect(): lax.ppermute(line, axis, [(d, (d - have) % ways) for d in range(ways)])]
  transfers between devices with their start and end apart: 5 -> 8, of which waited for: 5 -> 7; matrix products, arithmetic and copies ran while one was open for 7% -> 8% of each run, Pallas kernels for 0% -> 0%
where the time goes in v1:
time: 347 us; the launch traced here: 346 us
  waiting for transfers between devices  238 us (69%)
  matrix products  48.8 us (14%)
  local copies, waits for them, and re-layouts  18.9 us (5%)
  other arithmetic  17.3 us (5%)
  between operations  15.2 us (4%)
  starting transfers between devices  8.38 us (2%)
    all_gather x1, waiting for transfers between devices, shards(): lax.all_gather(stacked, 'wide', axis=1, tiled=True)  125 us
    all_gather x1, waiting for transfers between devices, shards(): lax.all_gather(expert_query, 'wide', axis=0, tiled=True)  42.8 us
    ppermute x4, waiting for transfers between devices, collect(): lax.ppermute(line, axis, [(d, (d - have) % ways) for d in range(ways)])  38.6 us
    all_gather x1, waiting for transfers between devices, shards(): lax.all_gather(expert_output, 'wide', axis=0, tiled=True)  29.6 us
    dot_general x1, matrix products, shards(): jnp.einsum('pd,kdc->pkc', normed, lax.all_gather(stacked, 'wide', axis=1,...  9.54 us
    ppermute x4, starting transfers between devices, collect(): lax.ppermute(line, axis, [(d, (d - have) % ways) for d in range(ways)])  8.26 us
    dot_general x4, matrix products, expert_steps(): jnp.dot(attn_mixed, output_w, preferred_element_type=jnp.float32)  7.42 us
  transfers between devices with their start and end apart: 8, of which 7 were waited for; matrix products, arithmetic and copies ran while one was open for 8% of the time, Pallas kernels for 0%

profile of v1, /device:TPU:0, one launch (start us, length us, event | category | flops | bytes accessed | tf_op | source)
XLA Modules:
  0.0 346.2 jit_solution(7345285925508017053)
XLA Ops:
  6.5 0.7 all-gather.9.cloned.1.call-update
  7.3 0.7 all-gather.7.cloned.1.call-update
  8.1 2.4 pad_maximum_fusion
  10.5 5.5 %collective-permute-start = (bf16[64,512]{1,0:T(8,128)(2,1)S(1)}, bf16[64,512]{1,0:T(8,128)(2,1)S(1)}, u32[]{:S(2)}, u32[]{:S(2)}) collective-permute-start(bf16[64,512]{1,0:T(8,128)(2,1)S(1)} %copy-done.22), channel_id=1, source_target_pairs={{0,15},{1,0},{2,1},{3,2},{4,3},{5,4},{6,5},{7,6},{8,7},{9,8},{10,9... | collective-permute-start | bytes 196616 | tf_op jit(solution)/shard_map/ppermute | solution.py:17
  16.4 3.1 fusion
  21.4 0.6 pad_maximum_fusion.5
  22.0 0.6 pad_maximum_fusion.6
  22.6 1.1 collective-permute-start.1
  23.7 0.6 pad_maximum_fusion.7
  24.3 3.4 collective-permute-done.1
  27.6 0.7 pad_maximum_fusion.2
  28.4 1.3 collective-permute-start.2
  29.7 6.7 %collective-permute-done.2 = bf16[256,512]{1,0:T(8,128)(2,1)S(1)} collective-permute-done((bf16[256,512]{1,0:T(8,128)(2,1)}, bf16[256,512]{1,0:T(8,128)(2,1)S(1)}, u32[]{:S(2)}, u32[]{:S(2)}) %collective-permute-start.2) | collective-permute-done | bytes 262176 | tf_op jit(solution)/shard_map/ppermute | solution.py:17
  37.0 28.6 %collective-permute-done.3 = bf16[512,512]{1,0:T(8,128)(2,1)S(1)} collective-permute-done((bf16[512,512]{1,0:T(8,128)(2,1)S(1)}, bf16[512,512]{1,0:T(8,128)(2,1)S(1)}, u32[]{:S(2)}, u32[]{:S(2)}) %collective-permute-start.3) | collective-permute-done | bytes 524320 | tf_op jit(solution)/shard_map/ppermute | solution.py:17
  66.0 0.9 reshape.309
  66.9 0.5 all-gather.9.cloned.1.call-done
  67.5 1.5 fusion.115
  69.2 42.8 %all-gather.7.cloned.1.call-done = bf16[1024,1024]{1,0:T(8,128)(2,1)} async-done(((bf16[64,1024]{1,0:T(8,128)(2,1)}), bf16[1024,1024]{1,0:T(8,128)(2,1)}) %all-gather.7.cloned.1.call-update) | async-done | bytes 2097168 | tf_op jit(solution)/shard_map/all_gather | solution.py:146
  112.0 2.1 fusion.114
  114.8 124.6 %all-gather.5.cloned.1.call-done = bf16[2,8192,512]{2,1,0:T(8,128)(2,1)} async-done(((bf16[2,512,512]{2,1,0:T(8,128)(2,1)}), bf16[2,8192,512]{2,1,0:T(8,128)(2,1)}) %all-gather.5.cloned.1.call-update) | async-done | bytes 16777232 | tf_op jit(solution)/shard_map/all_gather | solution.py:158
  239.4 9.5 %fusion.4 = f32[256,2,512]{2,0,1:T(8,128)S(1)} fusion(bf16[2,8192,512]{2,1,0:T(8,128)(2,1)} %all-gather.5.cloned.1.call-done, bf16[1,256,8192]{2,1,0:T(8,128)(2,1)} %param.14, f32[8192]{0:T(1024)S(1)} %copy-done.52, f32[256]{0:T(256)S(1)} %add_rsqrt_fusion), kind=kOutput, calls=%fused_computation.6 | convolution fusion | flops 4303355904 | bytes 22053888 | tf_op jit(solution)/shard_map/pd,kdc->pkc/dot_general | solution.py:155
  251.5 29.6 %all-gather.11.cloned.1.call-done = bf16[1024,1024]{1,0:T(8,128)(2,1)} async-done(((bf16[64,1024]{1,0:T(8,128)(2,1)}), bf16[1024,1024]{1,0:T(8,128)(2,1)}) %all-gather.11.cloned.1.call-update) | async-done | bytes 2097168 | tf_op jit(solution)/shard_map/all_gather | solution.py:149
  281.1 2.2 multiply_reduce_fusion.6
  284.2 2.2 convolution_convert_fusion.2
  287.2 0.6 copy-done.27
  287.9 1.7 fusion.108
  289.5 0.9 fusion.117
  290.5 1.6 reshape.311
  292.1 1.1 fusion.104
  293.1 0.8 subtract_convert_fusion.3
  293.9 1.2 fusion.109
  295.1 0.7 max.29
  295.9 1.3 fusion.31
  297.3 0.6 copy-done.51
  297.8 2.1 fusion.35
  299.9 1.4 reshape.312
  301.4 1.3 fusion.19
  302.7 0.7 copy.50
  303.4 1.6 convert_element_type.174
  305.0 2.3 multiply_reduce_fusion.4
  308.3 0.6 copy-done.20
  309.0 0.9 convolution_convert_fusion.1
  310.8 0.6 copy-done.28
  311.5 1.1 fusion.110
  312.5 0.9 fusion.119
  313.5 1.6 reshape.314
  315.0 1.1 fusion.103
  316.1 0.8 subtract_convert_fusion.2
  316.9 1.2 fusion.111
  318.2 1.4 fusion.32
  319.6 2.1 fusion.36
  321.7 1.4 reshape.315
  323.1 1.3 fusion.18
  324.5 0.7 copy.57
  325.2 1.6 convert_element_type.184
  326.8 2.3 multiply_reduce_fusion.2
  329.1 1.0 fusion.23
  330.1 1.2 multiply_reduce_fusion.1
  331.3 0.7 copy-done.17
  332.0 0.8 multiply_convert_fusion.1
  332.8 0.9 convolution_convert_fusion
  336.3 1.5 fusion.37
  338.2 0.6 multiply_reduce_fusion
  338.8 0.8 fusion.22
  (211 shorter events, 12.1 us)
Async XLA Ops:
  6.5 13.5 %copy-start = (f32[32,1024]{1,0:T(8,128)S(1)}, f32[32,1024]{1,0:T(8,128)}, u32[]{:S(2)}) copy-start(f32[32,1024]{1,0:T(8,128)} %param.20) | copy-start | bytes 393220
  6.5 4.0 %copy-start.22 = (bf16[64,512]{1,0:T(8,128)(2,1)S(1)}, bf16[64,512]{1,0:T(8,128)(2,1)}, u32[]{:S(2)}) copy-start(bf16[64,512]{1,0:T(8,128)(2,1)} %param.24) | copy-start | bytes 196612
  6.5 60.9 %all-gather.9.cloned.1.call-start = ((), (), s32[]{:S(2)}) async-start(), calls=%async_computation.2 | async-start | bytes 1114112 | tf_op jit(solution)/shard_map/all_gather | solution.py:147
  7.3 104.7 %all-gather.7.cloned.1.call-start = ((), (), s32[]{:S(2)}) async-start(), calls=%async_computation.1 | async-start | bytes 2228224 | tf_op jit(solution)/shard_map/all_gather | solution.py:146
  8.0 231.4 %all-gather.5.cloned.1.call-start = ((), (), s32[]{:S(2)}) async-start(), calls=%async_computation | async-start | bytes 17825792 | tf_op jit(solution)/shard_map/all_gather | solution.py:158
  10.5 270.6 %all-gather.11.cloned.1.call-start = ((), (), s32[]{:S(2)}) async-start(), calls=%async_computation.3 | async-start | bytes 2228224 | tf_op jit(solution)/shard_map/all_gather | solution.py:149
  10.5 12.1 %collective-permute-start = (bf16[64,512]{1,0:T(8,128)(2,1)S(1)}, bf16[64,512]{1,0:T(8,128)(2,1)S(1)}, u32[]{:S(2)}, u32[]{:S(2)}) collective-permute-start(bf16[64,512]{1,0:T(8,128)(2,1)S(1)} %copy-done.22), channel_id=1, source_target_pairs={{0,15},{1,0},{2,1},{3,2},{4,3},{5,4},{6,5},{7,6},{8,7},{9,8},{10,9... | collective-permute-start | bytes 196616 | tf_op jit(solution)/shard_map/ppermute | solution.py:17
  16.3 3.7 %copy-start.38 = (f32[1,50,32]{1,2,0:T(8,128)S(1)}, f32[1,50,32]{1,2,0:T(8,128)}, u32[]{:S(2)}) copy-start(f32[1,50,32]{1,2,0:T(8,128)} %param.16) | copy-start | bytes 19204
  16.4 13.3 %copy-start.35 = (f32[1024]{0:T(1024)S(1)}, f32[1024]{0:T(1024)}, u32[]{:S(2)}) copy-start(f32[1024]{0:T(1024)} %param.21) | copy-start | bytes 12292
  21.4 92.8 %copy-start.7 = (f32[50,64]{1,0:T(8,128)}, f32[50,64]{1,0:T(8,128)S(1)}, u32[]{:S(2)}) copy-start(f32[50,64]{1,0:T(8,128)S(1)} %get-tuple-element.33) | copy-start | bytes 38404
  21.4 92.8 %copy-start.12 = (f32[50,64]{1,0:T(8,128)}, f32[50,64]{1,0:T(8,128)S(1)}, u32[]{:S(2)}) copy-start(f32[50,64]{1,0:T(8,128)S(1)} %get-tuple-element.34) | copy-start | bytes 38404
  22.6 5.0 %collective-permute-start.1 = (bf16[128,512]{1,0:T(8,128)(2,1)S(1)}, bf16[128,512]{1,0:T(8,128)(2,1)S(1)}, u32[]{:S(2)}, u32[]{:S(2)}) collective-permute-start(bf16[128,512]{1,0:T(8,128)(2,1)S(1)} %pad_maximum_fusion.3), channel_id=1, source_target_pairs={{0,14},{1,15},{2,0},{3,1},{4,2},{5,3},{6,4},{7,5},{8,6},{9,7},{10,... | collective-permute-start | bytes 393224 | tf_op jit(solution)/shard_map/ppermute | solution.py:17
  28.4 8.1 %collective-permute-start.2 = (bf16[256,512]{1,0:T(8,128)(2,1)}, bf16[256,512]{1,0:T(8,128)(2,1)S(1)}, u32[]{:S(2)}, u32[]{:S(2)}) collective-permute-start(bf16[256,512]{1,0:T(8,128)(2,1)} %pad_maximum_fusion.2), channel_id=1, source_target_pairs={{0,12},{1,13},{2,14},{3,15},{4,0},{5,1},{6,2},{7,3},{8,4},{9,5},{1... | collective-permute-start | bytes 786440 | tf_op jit(solution)/shard_map/ppermute | solution.py:17
  29.6 220.3 %copy-start.47 = (pred[256]{0:T(512)(128)(4,1)}, pred[256]{0:T(512)(128)(4,1)S(1)}, u32[]{:S(2)}) copy-start(pred[256]{0:T(512)(128)(4,1)S(1)} %iota_compare_fusion) | copy-start | bytes 772
  36.5 29.1 %collective-permute-start.3 = (bf16[512,512]{1,0:T(8,128)(2,1)S(1)}, bf16[512,512]{1,0:T(8,128)(2,1)S(1)}, u32[]{:S(2)}, u32[]{:S(2)}) collective-permute-start(bf16[512,512]{1,0:T(8,128)(2,1)S(1)} %pad_maximum_fusion.1), channel_id=1, source_target_pairs={{0,8},{1,9},{2,10},{3,11},{4,12},{5,13},{6,14},{7,15},{8,0},{9,1},... | collective-permute-start | bytes 1572872 | tf_op jit(solution)/shard_map/ppermute | solution.py:17
  65.7 48.4 %copy-start.4 = (bf16[2048,512]{1,0:T(8,128)(2,1)}, bf16[2048,512]{1,0:T(8,128)(2,1)S(1)}, u32[]{:S(2)}) copy-start(bf16[2048,512]{1,0:T(8,128)(2,1)S(1)} %constant_dynamic-update-slice_fusion) | copy-start | bytes 6291460
  69.2 170.2 %copy-start.52 = (f32[8192]{0:T(1024)S(1)}, f32[8192]{0:T(1024)}, u32[]{:S(2)}) copy-start(f32[8192]{0:T(1024)} %param.17) | copy-start | bytes 98308
  249.3 1.4 copy-start.31
  250.0 1.1 copy-start.43
  251.0 32.2 %copy-start.23 = (bf16[1024,32]{0,1:T(8,128)(2,1)S(1)}, bf16[1024,32]{0,1:T(8,128)(2,1)}, u32[]{:S(2)}) copy-start(bf16[1024,32]{0,1:T(8,128)(2,1)} %param.27) | copy-start | bytes 196612
  251.1 32.2 %copy-start.39 = (f32[1,50,32]{1,2,0:T(8,128)S(1)}, f32[1,50,32]{1,2,0:T(8,128)}, u32[]{:S(2)}) copy-start(f32[1,50,32]{1,2,0:T(8,128)} %param.16) | copy-start | bytes 19204
  251.1 32.2 %copy-start.40 = (f32[1024]{0:T(1024)S(1)}, f32[1024]{0:T(1024)}, u32[]{:S(2)}) copy-start(f32[1024]{0:T(1024)} %param.26) | copy-start | bytes 12292
  251.1 32.4 %copy-start.46 = (f32[1024]{0:T(1024)S(1)}, f32[1024]{0:T(1024)}, u32[]{:S(2)}) copy-start(f32[1024]{0:T(1024)} %pad_maximum_fusion.5) | copy-start | bytes 12292
  251.3 32.7 %copy-start.36 = (f32[1024]{0:T(1024)S(1)}, f32[1024]{0:T(1024)}, u32[]{:S(2)}) copy-start(f32[1024]{0:T(1024)} %param.21) | copy-start | bytes 12292
  251.5 34.8 %copy-start.1 = (bf16[1024,1024]{1,0:T(8,128)(2,1)S(1)}, bf16[1024,1024]{1,0:T(8,128)(2,1)}, u32[]{:S(2)}) copy-start(bf16[1024,1024]{1,0:T(8,128)(2,1)} %all-gather.7.cloned.1.call-done) | copy-start | bytes 6291460
  284.0 2.3 copy-start.19
  284.2 2.7 copy-start.8
  284.2 2.7 copy-start.13
  286.3 1.5 copy-start.48
  286.8 2.7 copy-start.3
  287.2 0.6 copy-start.27
  295.1 2.0 copy-start.29
  295.9 1.4 copy-start.44
  297.2 0.6 copy-start.51
  305.0 2.4 copy-start.24
  305.0 2.4 copy-start.41
  305.0 2.6 copy-start.45
  305.0 3.9 %copy-start.37 = (f32[1024]{0:T(1024)S(1)}, f32[1024]{0:T(1024)}, u32[]{:S(2)}) copy-start(f32[1024]{0:T(1024)} %param.21) | copy-start | bytes 12292
  305.0 3.9 %copy-start.5 = (bf16[2048,512]{1,0:T(8,128)(2,1)S(1)}, bf16[2048,512]{1,0:T(8,128)(2,1)}, u32[]{:S(2)}) copy-start(bf16[2048,512]{1,0:T(8,128)(2,1)} %copy-done.4) | copy-start | bytes 6291460
  307.7 0.6 copy-start.34
  308.2 0.7 copy-start.20
  309.0 1.5 copy-start.9
  309.0 1.5 copy-start.14
  309.9 1.5 copy-start.49
  310.8 0.6 copy-start.28
  318.1 1.4 copy-start.30
  326.8 2.4 copy-start.25
  326.8 6.0 %copy-start.6 = (bf16[2048,512]{1,0:T(8,128)(2,1)S(1)}, bf16[2048,512]{1,0:T(8,128)(2,1)}, u32[]{:S(2)}) copy-start(bf16[2048,512]{1,0:T(8,128)(2,1)} %copy-done.4) | copy-start | bytes 6291460
  331.3 0.7 copy-start.17
  332.8 1.5 copy-start.10
  332.8 1.5 copy-start.15
  333.7 0.9 copy-start.50
  334.3 1.2 copy-start.11
  334.3 1.2 copy-start.16
  335.0 0.8 copy-start.21
  335.0 1.2 copy-start.32
  335.4 2.4 copy-start.33
  336.2 2.0 copy-start.2
  336.2 2.0 copy-start.18
  337.7 1.1 copy-start.26
  337.8 1.1 copy-start.42
Sparse Core Ops, SparseCore 0:
  9.5 57.9 all-gather.8
  69.6 42.3 all-gather.6
  114.2 125.1 all-gather.4
  241.4 39.6 all-gather.10
